TPU v7x, 32 devices: a whole 2x2x4 slice. The times are simulated.
32 devices in a mesh: grp: 2 (over y), row: 8 (over z, x), col: 2 (over core).
Axes of the slice: x: 2, y: 2, z: 4, core: 2. Of those that a mesh axis runs over, the one named last changes fastest.
Arguments:
- normed_features: bfloat16 [64, 32, 256], P(('grp', 'col'), 'row'), parts along dimension 0, may hold values from -6 to 6
- alignment_mask: int32 [64, 32], P(('grp', 'col'), 'row'), parts along dimension 0, may hold values from 0 to 1, as said below
- residue_present_mask: int32 [64], P(('grp', 'row')), parts along dimension 0, may hold values from 0 to 1
- first_factor_matrix: bfloat16 [256, 32], replicated, may hold values from -0.375 to 0.375
- second_factor_matrix: bfloat16 [256, 32], replicated, may hold values from -0.375 to 0.375
- output_weight: bfloat16 [1024, 128], replicated, may hold values from -0.75 to 0.75
- pairwise_bias: float32 [128], replicated, may hold values from -3 to 3
- cotangent: bfloat16 [64, 32, 128], P(('grp', 'row'), 'col'), parts along dimension 0, may hold values from -0.72 to 0.72
Outputs:
- pair_update: bfloat16 [64, 32, 128], P(('grp', 'row'), 'col'), parts along dimension 0
- left_grad: float32 [64, 32, 32], P(('grp', 'col'), 'row'), parts along dimension 0
- right_grad: float32 [64, 32, 32], P(('grp', 'col'), 'row'), parts along dimension 0
There are 2 independent parts, one for each index of `grp`. A program takes and returns all parts, laid end to end along the dimension named above; an argument that names none is the same for every part. Nothing has to cross between parts.
Inputs may be any that keep to these rules, and one draw needn't show every extreme that they name: `alignment_mask`: 0 or 1; sequence 0 (the query) is present at every residue.
All inputs are finite; a program needn't handle non-finite values.
Results may differ from a plain program's by a relative error of at most 0.006.
Values may be sent and summed in bfloat16 or wider, within the bound.
A program may use at most 64 MiB of HBM per device.

v0:
```python
import math

import jax
import jax.numpy as jnp
from jax import lax
from jax.sharding import PartitionSpec as P


def per_device(
    normed_features,
    alignment_mask,
    residue_present_mask,
    first_factor_matrix,
    second_factor_matrix,
    output_weight,
    pairwise_bias,
    cotangent,
):
    sequence_halfway = normed_features.shape[0]
    residue_local = normed_features.shape[1]
    alignment_width = normed_features.shape[2]
    proj_width = first_factor_matrix.shape[1]
    res_half = cotangent.shape[1]
    channels = output_weight.shape[1]
    present_entry_mask = (
        alignment_mask.astype(jnp.float32) * residue_present_mask.astype(jnp.float32)[None, :]
    )
    flattened_row_list = normed_features.reshape(sequence_halfway * residue_local, alignment_width)
    left_own = jnp.dot(
        flattened_row_list, first_factor_matrix, preferred_element_type=jnp.float32
    ).reshape(sequence_halfway, residue_local, proj_width)
    left_own = (left_own * present_entry_mask[:, :, None]).astype(jnp.bfloat16)
    right_own = jnp.dot(
        flattened_row_list, second_factor_matrix, preferred_element_type=jnp.float32
    ).reshape(sequence_halfway, residue_local, proj_width)
    right_own = (right_own * present_entry_mask[:, :, None]).astype(jnp.bfloat16)
    mask_half = present_entry_mask.astype(jnp.bfloat16)
    left_all, left_mask = (
        lax.all_gather(left_own, "col", axis=0, tiled=True),
        lax.all_gather(mask_half, "col", axis=0, tiled=True),
    )
    column = lax.axis_index("col")
    right_seq, mask_seq = (
        lax.all_gather(right_own, "col", axis=0, tiled=True),
        lax.all_gather(mask_half, "col", axis=0, tiled=True),
    )
    right_res, mask_res = (
        lax.all_gather(right_seq, "row", axis=1, tiled=True),
        lax.all_gather(mask_seq, "row", axis=1, tiled=True),
    )
    right_cols = lax.dynamic_slice_in_dim(right_res, column * res_half, res_half, 1)
    mask_cols = lax.dynamic_slice_in_dim(mask_res, column * res_half, res_half, 1)
    sequence_count = left_all.shape[0]
    pair_count = lax.dot_general(
        left_mask, mask_cols, (((0,), (0,)), ((), ())), preferred_element_type=jnp.float32
    )
    divisor = jnp.maximum(pair_count, 1.0)
    col_block = math.gcd(res_half, 128)
    num_blocks = res_half // col_block

    def per_block(running, block_idx):
        offset = block_idx * col_block
        right_blk = lax.dynamic_slice_in_dim(right_cols, offset, col_block, 1)
        div_blk = lax.dynamic_slice_in_dim(divisor, offset, col_block, 1)
        cot_blk = lax.dynamic_slice_in_dim(cotangent, offset, col_block, 1)
        products = jnp.einsum(
            "sic,sje->ijce", left_all, right_blk, preferred_element_type=jnp.float32
        ).astype(jnp.bfloat16)
        products = products.reshape(residue_local * col_block, proj_width * proj_width)
        mapped = jnp.dot(products, output_weight, preferred_element_type=jnp.float32).reshape(
            residue_local, col_block, channels
        )
        pair_blk = (mapped / div_blk[:, :, None] + pairwise_bias[None, None, :]).astype(
            jnp.bfloat16
        )
        scaled = (
            (cot_blk.astype(jnp.float32) / div_blk[:, :, None])
            .astype(jnp.bfloat16)
            .reshape(residue_local * col_block, channels)
        )
        grad_outer = lax.dot_general(
            scaled, output_weight, (((1,), (1,)), ((), ())), preferred_element_type=jnp.float32
        )
        grad_outer = grad_outer.astype(jnp.bfloat16).reshape(
            residue_local, col_block, proj_width, proj_width
        )
        left_term = jnp.einsum(
            "ijce,sje->sic", grad_outer, right_blk, preferred_element_type=jnp.float32
        )
        right_term = jnp.einsum(
            "ijce,sic->sje", grad_outer, left_all, preferred_element_type=jnp.float32
        )
        return (running + left_term, (pair_blk, right_term))

    start_grad = jnp.zeros((sequence_count, residue_local, proj_width), jnp.float32)
    left_sum, (pairs, right_terms) = lax.scan(
        per_block, start_grad, jnp.arange(num_blocks, dtype=jnp.int32)
    )
    pair_update = jnp.moveaxis(pairs, 0, 1).reshape(residue_local, res_half, channels)
    right_part = jnp.moveaxis(right_terms, 0, 1).reshape(sequence_count, res_half, proj_width)
    left_grad = lax.psum_scatter(left_sum, "col", scatter_dimension=0, tiled=True)
    right_total = lax.psum(right_part, "row")
    first_res = lax.axis_index("row") * residue_local
    owner_half = first_res // res_half
    picked = lax.dynamic_slice_in_dim(
        right_total, first_res - owner_half * res_half, residue_local, 1
    )
    picked = jnp.where(owner_half == column, picked, jnp.zeros_like(picked))
    right_grad = lax.psum_scatter(picked, "col", scatter_dimension=0, tiled=True)
    return (pair_update, left_grad, right_grad)


def solution(mesh):
    placed = (
        P(("grp", "col"), "row", None),
        P(("grp", "col"), "row"),
        P(("grp", "row")),
        P(),
        P(),
        P(),
        P(),
        P(("grp", "row"), "col", None),
    )
    return jax.shard_map(
        per_device,
        mesh=mesh,
        in_specs=placed,
        out_specs=(
            P(("grp", "row"), "col", None),
            P(("grp", "col"), "row", None),
            P(("grp", "col"), "row", None),
        ),
        check_vma=False,
    )
```

profile of v0, /device:TPU:0, one launch (start us, length us, event | category | flops | bytes accessed | tf_op | source)
XLA Modules:
  0.0 123.4 jit_solution(13162910336298129301)
XLA Ops:
  8.1 0.7 copy-done.7
  8.9 1.9 %all-gather = bf16[2,16,4]{1,2,0:T(4,128)(2,1)S(1)} all-gather(bf16[1,16,4]{1,2,0:T(4,128)(2,1)S(1)} %get-tuple-element.42), channel_id=1, replica_groups=mesh['grp'=2,'row'=8,'col'=2] {'col'}, dimensions={0}, use_global_device_ids=true | all-gather | bytes 384 | tf_op jit(solution)/shard_map/all_gather | solution.py:40
  10.8 0.1 reshape.36
  10.9 22.1 %all-gather.1 = bf16[8,4,32]{2,1,0:T(4,128)(2,1)S(1)} all-gather(bf16[1,4,32]{2,1,0:T(4,128)(2,1)S(1)} %bitcast.55), channel_id=1, replica_groups=mesh['grp'=2,'row'=8,'col'=2] {'row'}, dimensions={0}, use_global_device_ids=true | all-gather | bytes 2304 | tf_op jit(solution)/shard_map/all_gather | solution.py:49
  33.0 0.9 fusion.3
  33.9 2.0 %all_gather.18 = bf16[32,4,32]{2,0,1:T(8,128)(2,1)S(1)} all-gather(bf16[16,4,32]{2,0,1:T(8,128)(2,1)S(1)} %fusion.3), channel_id=1, replica_groups=mesh['grp'=2,'row'=8,'col'=2] {'col'}, dimensions={0}, use_global_device_ids=true | all-gather | bytes 12288 | tf_op jit(solution)/shard_map/all_gather | solution.py:39
  35.9 0.1 convolution_maximum_fusion
  36.1 0.2 convolution_convert_fusion.1
  36.3 0.4 reshape.34
  36.7 1.0 convolution_bitcast_fusion
  37.7 0.7 copy-done.4
  38.5 1.9 %all_gather.16 = bf16[32,4,32]{2,0,1:T(8,128)(2,1)S(1)} all-gather(bf16[16,4,32]{2,0,1:T(8,128)(2,1)S(1)} %fusion.2), channel_id=1, replica_groups=mesh['grp'=2,'row'=8,'col'=2] {'col'}, dimensions={0}, use_global_device_ids=true | all-gather | bytes 12288 | tf_op jit(solution)/shard_map/all_gather | solution.py:44
  40.4 30.8 %all_gather.17 = bf16[32,32,32]{2,0,1:T(8,128)(2,1)S(1)} all-gather(bf16[32,4,32]{2,0,1:T(8,128)(2,1)S(1)} %all_gather.16), channel_id=1, replica_groups=mesh['grp'=2,'row'=8,'col'=2] {'row'}, dimensions={1}, use_global_device_ids=true | all-gather | bytes 73728 | tf_op jit(solution)/shard_map/all_gather | solution.py:48
  71.2 1.1 convolution_bitcast_fusion.1
  72.4 0.3 fusion
  72.7 0.3 copy.29
  73.0 0.5 dot_general.34
  73.5 32.8 %all-reduce.2.cloned.1.call-done = f32[32,16,32]{2,0,1:T(8,128)} async-done(((f32[32,16,32]{2,0,1:T(8,128)}), f32[32,16,32]{2,0,1:T(8,128)}) %all-reduce.2.cloned.1.call-update) | async-done | bytes 65552 | tf_op jit(solution)/shard_map/psum | solution.py:102
  106.3 1.5 %dynamic-slice_select_fusion = f32[32,4,32]{2,0,1:T(8,128)} fusion(f32[32,16,32]{2,0,1:T(8,128)} %all-reduce.2.cloned.1.call-done, s32[]{:T(128)S(6)} %select_n.27, pred[]{:T(512)S(6)} %eq.3), kind=kLoop, calls=%fused_computation.18 | loop fusion | flops 4096 | bytes 32773 | tf_op jit(solution)/shard_map/jit(_where)/select_n | solution.py:108
  107.8 0.6 copy-done.3
  108.5 0.8 fusion.4
  109.2 1.4 %copy.33 = f32[16,4,32]{2,1,0:T(4,128)} copy(f32[16,4,32]{2,0,1:T(8,128)} %reduce-scatter.3.cloned.1.call-done) | data formatting | bytes 16384
  110.6 4.0 %reduce-scatter.5.cloned.1.call-done = f32[16,4,32]{2,0,1:T(8,128)} async-done(((f32[32,4,32]{2,0,1:T(8,128)}), f32[16,4,32]{2,0,1:T(8,128)}) %reduce-scatter.5.cloned.1.call-update) | async-done | bytes 8208 | tf_op jit(solution)/shard_map/reduce_scatter | solution.py:109
  114.6 1.4 %copy.34 = f32[16,4,32]{2,1,0:T(4,128)} copy(f32[16,4,32]{2,0,1:T(8,128)} %reduce-scatter.5.cloned.1.call-done) | data formatting | bytes 16384
  (25 shorter events, 0.5 us)
Async XLA Ops:
  8.0 28.1 %copy-start = (bf16[1024,128]{1,0:T(8,128)(2,1)S(1)}, bf16[1024,128]{1,0:T(8,128)(2,1)}, u32[]{:S(2)}) copy-start(bf16[1024,128]{1,0:T(8,128)(2,1)} %param.13) | copy-start | bytes 786436
  8.0 98.3 %all-reduce.2.cloned.1.call-start = ((), (), s32[]{:S(2)}) async-start(), calls=%async_computation.3 | async-start | bytes 524288 | tf_op jit(solution)/shard_map/psum | solution.py:102
  8.1 0.7 copy-start.7
  8.1 0.7 copy-start.2
  8.8 24.3 %copy-start.5 = (bf16[256,32]{0,1:T(8,128)(2,1)S(1)}, bf16[256,32]{0,1:T(8,128)(2,1)}, u32[]{:S(2)}) copy-start(bf16[256,32]{0,1:T(8,128)(2,1)} %param.11) | copy-start | bytes 49156
  33.9 2.1 %copy-start.1 = (bf16[4,16,128]{2,1,0:T(8,128)(2,1)S(1)}, bf16[4,16,128]{2,1,0:T(8,128)(2,1)}, u32[]{:S(2)}) copy-start(bf16[4,16,128]{2,1,0:T(8,128)(2,1)} %param.15) | copy-start | bytes 49156
  37.7 0.8 copy-start.4
  37.7 0.8 copy-start.6
  37.7 71.5 %reduce-scatter.3.cloned.1.call-start = ((), (), s32[]{:S(2)}) async-start(), calls=%async_computation.2 | async-start | bytes 98304 | tf_op jit(solution)/shard_map/reduce_scatter | solution.py:101
  72.3 42.3 %reduce-scatter.5.cloned.1.call-start = ((), (), s32[]{:S(2)}) async-start(), calls=%async_computation.4 | async-start | bytes 98304 | tf_op jit(solution)/shard_map/reduce_scatter | solution.py:109
  107.8 0.7 copy-start.3
Sparse Core Ops, SparseCore 0:
  37.8 68.4 all-reduce.1
Sparse Core Ops, SparseCore 1:
  72.4 4.7 reduce-scatter.2
  107.9 6.6 reduce-scatter.4
where the time goes:
time: 124 us; the launch traced here: 123 us
  blocking collectives  58.7 us (47%)
  waiting for transfers between devices  36.8 us (30%)
  between operations  15.6 us (13%)
  local copies, waits for them, and re-layouts  6.08 us (5%)
  matrix products  4.44 us (4%)
  other arithmetic  1.62 us (1%)
    psum x1, waiting for transfers between devices, per_device(): right_total = lax.psum(right_part, 'row')  32.8 us
    all_gather x1, blocking collectives, per_device(): lax.all_gather(right_seq, 'row', axis=1, tiled=True)  30.8 us
    all_gather x1, blocking collectives, per_device(): lax.all_gather(mask_seq, 'row', axis=1, tiled=True)  22.1 us
    unnamed x19, local copies, waits for them, and re-layouts  4.9 us
    reduce_scatter x1, waiting for transfers between devices, per_device(): lax.psum_scatter(picked, 'col', scatter_dimension=0, tiled=True)  3.99 us
  transfers between devices with their start and end apart: 3, of which 2 were waited for; matrix products, arithmetic and copies ran while one was open for 5% of the time, Pallas kernels for 0%

commit v1 on v0

v1 whole, which is shorter than its diff:
```python
import functools

import jax
import jax.numpy as jnp
from jax import lax
from jax.experimental import pallas as pl
from jax.experimental.pallas import tpu as pltpu
from jax.sharding import PartitionSpec as P

F32 = jnp.float32
BF16 = jnp.bfloat16
MESH = pl.DeviceIdType.MESH
UNROLL = 8


def iota(shape, axis):
    return lax.broadcasted_iota(jnp.int32, shape, axis)


def mm(a, b):
    return lax.dot_general(a, b, (((1,), (0,)), ((), ())), preferred_element_type=F32)


def each(n, f):
    if n <= UNROLL:
        for k in range(n):
            f(k)
    else:

        @pl.loop(0, n)
        def _(k):
            f(k)


def kernel(
    nrow,
    x_ref, am_ref, rm_ref, wl_ref, wr_ref, w_ref, bias_ref, cot_ref,
    pu_ref, lg_ref, rg_ref,
    g_s, gp_r, f_s, l_r, r_r, ro_r, ct_s, ct_r, cf_r, m_s, m_r,
    w32, a32, b32, o32, c32, p2, q2,
    ssem, rsem, psem,
):
    seq, loc, feat = x_ref.shape
    proj = wl_ref.shape[1]
    half_res, chan = cot_ref.shape[1], cot_ref.shape[2]
    res = nrow * loc
    per_half = half_res // loc
    tiles = proj * seq // 128
    rows = loc * seq
    lo = loc.bit_length() - 1
    sq = seq.bit_length() - 1
    tl = tiles.bit_length() - 1

    grp, row, col = lax.axis_index("grp"), lax.axis_index("row"), lax.axis_index("col")
    other = 1 - col

    def half_of(r):
        return jnp.where(r >= per_half, 1, 0)

    def dev(r, c):
        return (grp, r, c)

    barrier = pltpu.get_barrier_semaphore()

    def greet(k):
        r = lax.rem(row + k, nrow)
        pl.semaphore_signal(barrier, inc=1, device_id=dev(r, other), device_id_type=MESH)
        if isinstance(k, int):
            if k:
                pl.semaphore_signal(barrier, inc=1, device_id=dev(r, col), device_id_type=MESH)
        else:

            @pl.when(k != 0)
            def _():
                pl.semaphore_signal(barrier, inc=1, device_id=dev(r, col), device_id_type=MESH)

    each(nrow, greet)

    xf = x_ref[...].astype(F32)
    x = jnp.concatenate([xf[:, r, :] for r in range(loc)], axis=0).astype(BF16)
    live = jnp.concatenate(
        [(am_ref[:, r : r + 1] * rm_ref[:, r : r + 1]).astype(F32) for r in range(loc)], axis=0
    )
    live = jnp.broadcast_to(live, (rows, 128))
    left = mm(x, wl_ref[...])
    right = mm(x, wr_ref[...])
    both = jnp.concatenate([left, right, jnp.ones((rows, 128 - 2 * proj), F32)], axis=1) * live
    g = both.astype(BF16)
    g_s[...] = g
    lane = iota((rows, 128), 1)
    at = iota((rows, 128), 0)
    m_s[...] = jnp.sum(jnp.where(lane == at, live, 0.0), axis=0, keepdims=True)
    width = 2 * proj * seq
    spread = (iota((128, width), 0) == (iota((128, width), 1) >> sq)).astype(BF16)
    own_seq = (iota((rows, width), 0) & (seq - 1)) == (iota((rows, width), 1) & (seq - 1))
    h = jnp.where(own_seq, mm(g, spread), 0.0).astype(BF16)
    h = jnp.concatenate([h[:, k * 128 : (k + 1) * 128] for k in range(2 * tiles)], axis=0)
    frows, deep = 2 * loc * tiles, 2 * tiles * rows
    fi, ki = iota((frows, deep), 0), iota((frows, deep), 1)
    f_x, f_r, f_t = fi >> (lo + tl), (fi >> tl) & (loc - 1), fi & (tiles - 1)
    k_x, k_t, k_r = ki >> (tl + lo + sq), (ki >> (lo + sq)) & (tiles - 1), (ki >> sq) & (loc - 1)
    pick = ((f_x == k_x) & (f_r == k_r) & (f_t == k_t)).astype(BF16)
    f = mm(pick, h).astype(BF16)
    fr = loc * tiles
    f_s[0] = f[:fr]
    f_s[1] = f[fr:]
    cot32 = cot_ref[...].astype(F32)
    for q in range(per_half if per_half <= UNROLL else 0):
        ct_s[q] = jnp.concatenate(
            [cot32[i, q * loc : (q + 1) * loc, :] for i in range(loc)], axis=0
        ).astype(BF16)
    if per_half > UNROLL:
        c32_rows = c32.shape[0] // loc

        for i in range(loc):
            c32[i * c32_rows : i * c32_rows + half_res] = cot32[i]

        @pl.loop(0, per_half)
        def _(q):
            ct_s[q] = jnp.concatenate(
                [
                    c32[pl.ds(i * c32_rows + q * loc, loc), :]
                    for i in range(loc)
                ],
                axis=0,
            ).astype(BF16)

    pl.semaphore_wait(barrier, 2 * nrow - 1)

    def copy(src, dst, kind, s_slot, r_slot, to):
        return pltpu.make_async_remote_copy(
            src_ref=src, dst_ref=dst, send_sem=ssem.at[kind, s_slot],
            recv_sem=rsem.at[kind, r_slot], device_id=to, device_id_type=MESH,
        )

    def partner(k):
        if k == 0:
            src, dst = g_s, gp_r
        else:
            src, dst = cot_ref, cf_r.at[:, pl.ds(pl.multiple_of(col * half_res, half_res), half_res), :]
        return pltpu.make_async_remote_copy(
            src_ref=src, dst_ref=dst, send_sem=psem.at[k], recv_sem=psem.at[2 + k],
            device_id=dev(row, other), device_id_type=MESH,
        )

    def on(pred, f):
        pl.when(pred)(f)

    def sends(k, act):
        r = lax.rem(row + k, nrow)
        q = jnp.where(r >= per_half, r - per_half, r)
        far = half_of(r) == col

        def same():
            act(copy(f_s.at[1], r_r.at[row], 1, r, row, dev(r, col)))
            act(copy(f_s.at[0], l_r.at[row], 0, r, row, dev(r, col)))
            act(copy(m_s, m_r.at[0, row], 4, r, row, dev(r, col)))
            on(far, lambda: act(copy(ct_s.at[q], ct_r.at[row], 3, r, row, dev(r, col))))

        if isinstance(k, int):
            if k:
                same()
        else:
            on(k != 0, same)
        on(
            half_of(row) == other,
            lambda: act(copy(f_s.at[1], ro_r.at[row], 2, r, row, dev(r, other))),
        )
        act(copy(m_s, m_r.at[1, row], 5, r, row, dev(r, other)))
        on(far, lambda: act(copy(ct_s.at[q], ct_r.at[row], 6, r, row, dev(r, other))))

    partner(0).start()
    partner(1).start()
    each(nrow, lambda j: sends(nrow - 1 - j, lambda d: d.start()))

    l_r[row] = f[:fr]
    r_r[row] = f[fr:]
    m_r[0, row] = m_s[...]
    cf_r[:, pl.ds(pl.multiple_of(col * half_res, half_res), half_res), :] = cot_ref[...]

    @pl.when(half_of(row) == col)
    def _():
        ct_r[row] = ct_s[jnp.where(row >= per_half, row - per_half, row)]

    w32[...] = w_ref[...].astype(F32)
    w_c = jnp.concatenate(
        [w32[pl.ds(e, proj, stride=proj), :] for e in range(proj)], axis=1
    ).astype(BF16)
    w_e = jnp.concatenate(
        [w_ref[c * proj : (c + 1) * proj, :] for c in range(proj)], axis=1
    )

    def spread_left(gl, part):
        p = mm(gl[:, :proj], w_c).astype(BF16)
        for e in range(proj):
            for i in range(loc):
                p2[part * proj * seq + e * seq : part * proj * seq + (e + 1) * seq,
                   i * chan : (i + 1) * chan] = p[
                    i * seq : (i + 1) * seq, e * chan : (e + 1) * chan
                ]

    spread_left(g, 0)
    partner(0).wait_recv()
    gp = gp_r[...]
    spread_left(gp, 1)

    def arrivals(k):
        r = lax.rem(row + nrow - k, nrow)

        def same():
            copy(f_s.at[1], r_r.at[r], 1, r, r, dev(r, col)).wait_recv()
            copy(f_s.at[0], l_r.at[r], 0, r, r, dev(r, col)).wait_recv()
            copy(m_s, m_r.at[0, r], 4, r, r, dev(r, col)).wait_recv()
            on(
                half_of(row) == col,
                lambda: copy(ct_s.at[0], ct_r.at[r], 3, r, r, dev(r, col)).wait_recv(),
            )

        if isinstance(k, int):
            if k:
                same()
        else:
            on(k != 0, same)
        on(
            half_of(r) == col,
            lambda: copy(f_s.at[1], ro_r.at[r], 2, r, r, dev(r, other)).wait_recv(),
        )
        copy(m_s, m_r.at[1, r], 5, r, r, dev(r, other)).wait_recv()
        on(
            half_of(row) == other,
            lambda: copy(ct_s.at[0], ct_r.at[r], 6, r, r, dev(r, other)).wait_recv(),
        )

    partner(1).wait_recv()
    each(nrow, arrivals)

    rep = (iota((res, nrow), 0) >> lo == iota((res, nrow), 1)).astype(BF16)
    own_lane = (iota((res, 128), 0) & (loc - 1)) == (iota((res, 128), 1) >> sq)
    z = [
        jnp.where(own_lane, mm(rep, m_r[k].reshape(nrow, 128).astype(BF16)), 0.0).astype(BF16)
        for k in range(2)
    ]
    counts = []
    for b in range(loc):
        total = None
        for k, gl in enumerate((g, gp)):
            m_b = jnp.broadcast_to(
                gl[b * seq : (b + 1) * seq, 2 * proj : 2 * proj + 1].astype(F32), (seq, 128)
            ).astype(BF16)
            term = mm(z[k], jnp.concatenate([m_b] * (128 // seq), axis=0))
            total = term if total is None else total + term
        counts.append(jnp.maximum(total, 1.0))

    def unflatten(ref, n, start=0):
        return jnp.concatenate(
            [ref[pl.ds(start + t, n, stride=tiles), :] for t in range(tiles)], axis=1
        ).astype(BF16)

    a32[...] = r_r[...].astype(F32).reshape(res * tiles, 128)
    b32[...] = l_r[...].astype(F32).reshape(res * tiles, 128)
    c32[...] = ct_r[...].astype(F32).reshape(res * loc, 128)
    o32[...] = (
        ro_r[pl.ds(col * per_half, per_half)].astype(F32).reshape(half_res * tiles, 128)
    )
    right_all = unflatten(a32, res)
    left_all = unflatten(b32, res)

    start = pl.multiple_of(col * half_res * tiles, half_res * tiles)
    r_half = jnp.concatenate(
        [unflatten(a32, half_res, start), unflatten(o32, half_res)], axis=1
    )
    mapped = mm(r_half, p2[...])
    bias = bias_ref[...]
    for i in range(loc):
        w32[:res] = counts[i]
        div = w32[pl.ds(pl.multiple_of(col * half_res, half_res), half_res), :]
        pu_ref[i] = (mapped[:, i * chan : (i + 1) * chan] / div + bias).astype(BF16)

    def grad(flat, scaled, weight):
        q = lax.dot_general(
            flat, scaled, (((0,), (0,)), ((), ())), preferred_element_type=F32
        ).astype(BF16)
        for e in range(proj):
            for i in range(loc):
                q2[i * seq : (i + 1) * seq, e * chan : (e + 1) * chan] = q[
                    e * seq : (e + 1) * seq, i * chan : (i + 1) * chan
                ]
        return lax.dot_general(
            q2[...], weight, (((1,), (1,)), ((), ())), preferred_element_type=F32
        )

    scaled = jnp.concatenate(
        [(cf_r[i].astype(F32) / counts[i]).astype(BF16) for i in range(loc)], axis=1
    )
    lg_ref[...] = grad(right_all, scaled, w_c)
    scaled_t = jnp.concatenate(
        [
            (c32[pl.ds(j, res, stride=loc), :] / counts[j]).astype(BF16)
            for j in range(loc)
        ],
        axis=1,
    )
    rg_ref[...] = grad(left_all, scaled_t, w_e)

    partner(0).wait_send()
    partner(1).wait_send()
    each(nrow, lambda j: sends(nrow - 1 - j, lambda d: d.wait_send()))


def per_device(nrow, x, am, rm, wl, wr, w, bias, cot):
    seq, loc, _ = x.shape
    proj = wl.shape[1]
    half_res, chan = cot.shape[1], cot.shape[2]
    res = nrow * loc
    tiles = proj * seq // 128
    fr = loc * tiles
    rows = loc * seq
    vm = pl.BlockSpec(memory_space=pltpu.VMEM)
    pu, lg, rg = pl.pallas_call(
        functools.partial(kernel, nrow),
        out_shape=(
            jax.ShapeDtypeStruct(cot.shape, BF16),
            jax.ShapeDtypeStruct((rows, proj), F32),
            jax.ShapeDtypeStruct((rows, proj), F32),
        ),
        in_specs=[vm] * 8,
        out_specs=(vm, vm, vm),
        scratch_shapes=[
            pltpu.VMEM((rows, 128), BF16),
            pltpu.VMEM((rows, 128), BF16),
            pltpu.VMEM((2, fr, 128), BF16),
            pltpu.VMEM((nrow, fr, 128), BF16),
            pltpu.VMEM((nrow, fr, 128), BF16),
            pltpu.VMEM((nrow, fr, 128), BF16),
            pltpu.VMEM((half_res // loc, loc * loc, 128), BF16),
            pltpu.VMEM((nrow, loc * loc, 128), BF16),
            pltpu.VMEM((loc, res, chan), BF16),
            pltpu.VMEM((1, 128), F32),
            pltpu.VMEM((2, nrow, 1, 128), F32),
            pltpu.VMEM((max(proj * proj, res), chan), F32),
            pltpu.VMEM((res * tiles, 128), F32),
            pltpu.VMEM((res * tiles, 128), F32),
            pltpu.VMEM((half_res * tiles, 128), F32),
            pltpu.VMEM((res * loc, 128), F32),
            pltpu.VMEM((2 * proj * seq, loc * chan), BF16),
            pltpu.VMEM((rows, proj * chan), BF16),
            pltpu.SemaphoreType.DMA((7, nrow)),
            pltpu.SemaphoreType.DMA((7, nrow)),
            pltpu.SemaphoreType.DMA((4,)),
        ],
        compiler_params=pltpu.CompilerParams(collective_id=0, has_side_effects=True),
    )(x, am, rm.reshape(1, loc), wl, wr, w, bias.reshape(1, chan), cot)
    lg = jnp.swapaxes(lg.reshape(loc, seq, proj), 0, 1)
    rg = jnp.swapaxes(rg.reshape(loc, seq, proj), 0, 1)
    return pu, lg, rg


def solution(mesh):
    placed = (
        P(("grp", "col"), "row", None),
        P(("grp", "col"), "row"),
        P(("grp", "row")),
        P(),
        P(),
        P(),
        P(),
        P(("grp", "row"), "col", None),
    )
    return jax.shard_map(
        functools.partial(per_device, mesh.shape["row"]),
        mesh=mesh,
        in_specs=placed,
        out_specs=(
            P(("grp", "row"), "col", None),
            P(("grp", "col"), "row", None),
            P(("grp", "col"), "row", None),
        ),
        check_vma=False,
    )
```

time: 124 us -> 20.7 us (0.17)
  blocking collectives: 58.7 us -> 0 us
  waiting for transfers between devices: 36.8 us -> 0 us
  between operations: 15.6 us -> 0.66 us
  Pallas kernels: 0 us -> 14.2 us
  matrix products: 4.44 us -> 0 us
  other arithmetic: 1.62 us -> 0 us
    all_gather x5 -> x0, blocking collectives: 58.7 us -> none  [the longest x1 30.8 us: per_device(): lax.all_gather(right_seq, 'row', axis=1, tiled=True)]
    psum x1 -> x0, waiting for transfers between devices: 32.8 us -> none  [per_device(): right_total = lax.psum(right_part, 'row')]
    pallas_call x0 -> x1, Pallas kernels: none -> 14.2 us  [per_device(): pl.pallas_call(functools.partial(kernel, nrow), out_shape=(jax.ShapeDtype...]
    dot_general x8 -> x0, matrix products: 4.44 us -> none  [the longest x1 1.07 us: per_block(): jnp.einsum('ijce,sje->sic', grad_outer, right_blk, preferred_element_type...]
    reduce_scatter x2 -> x0, waiting for transfers between devices: 3.99 us -> none  [the longest x1 3.99 us: per_device(): lax.psum_scatter(picked, 'col', scatter_dimension=0, tiled=True)]
    select_n x1 -> x0, other arithmetic: 1.46 us -> none  [per_device(): picked = jnp.where(owner_half == column, picked, jnp.zeros_like(picked))]
    transpose x0 -> x1, local copies, waits for them, and re-layouts: none -> 1.42 us  [per_device(): rg = jnp.swapaxes(rg.reshape(loc, seq, proj), 0, 1)]
    unnamed x19 -> x10, local copies, waits for them, and re-layouts: 4.9 us -> 4.15 us
  transfers between devices with their start and end apart: 3 -> 0, of which waited for: 2 -> 0; matrix products, arithmetic and copies ran while one was open for 5% -> 0% of each run, Pallas kernels for 0% -> 0%
where the time goes in v1:
time: 20.7 us; the launch traced here: 20.4 us
  Pallas kernels  14.2 us (69%)
  local copies, waits for them, and re-layouts  5.58 us (27%)
  between operations  0.66 us (3%)
    pallas_call x1, Pallas kernels, per_device(): pl.pallas_call(functools.partial(kernel, nrow), out_shape=(jax.ShapeDtype...  14.2 us
    unnamed x10, local copies, waits for them, and re-layouts  4.15 us
    transpose x1, local copies, waits for them, and re-layouts, per_device(): rg = jnp.swapaxes(rg.reshape(loc, seq, proj), 0, 1)  1.42 us

profile of v1, /device:TPU:0, one launch (start us, length us, event | category | flops | bytes accessed | tf_op | source)
XLA Modules:
  0.0 20.4 jit_solution(1290067452241233884)
XLA Ops:
  0.6 0.0 copy-start.2
  0.6 0.7 %copy-done.2 = s32[16,4]{0,1:T(4,128)S(1)} copy-done((s32[16,4]{0,1:T(4,128)S(1)}, s32[16,4]{0,1:T(4,128)}, u32[]{:S(2)}) %copy-start.2) | copy-done | bytes 280
  1.3 0.7 %copy.11.am_ref = s32[16,4]{1,0:T(8,128)} copy(s32[16,4]{0,1:T(4,128)S(1)} %copy-done.2) | data formatting | bytes 512 | tf_op args[1]
  2.0 0.0 copy-start
  2.0 1.5 %copy.12.wl_ref = bf16[256,32]{1,0:T(8,128)(2,1)} copy(bf16[256,32]{0,1:T(8,128)(2,1)} %param.11) | data formatting | bytes 32768 | tf_op args[3]
  3.4 0.0 copy-done
  3.5 0.7 %copy.13.wr_ref = bf16[256,32]{1,0:T(8,128)(2,1)} copy(bf16[256,32]{0,1:T(8,128)(2,1)S(1)} %copy-done) | data formatting | bytes 32768 | tf_op args[4]
  4.2 14.2 %shard_map.103 = (bf16[4,16,128]{2,1,0:T(8,128)(2,1)}, f32[64,32]{1,0:T(8,128)}, f32[64,32]{1,0:T(8,128)}) custom-call(bf16[16,4,256]{2,1,0:T(4,128)(2,1)} %x_ref.1, s32[16,4]{1,0:T(8,128)} %copy.11.am_ref, s32[1,4]{1,0:T(1,128)} %bitcast.10, bf16[256,32]{1,0:T(8,128)(2,1)} %copy.12.wl_ref, bf16[256,32]{1,0:T(8,128)(2,1)} %copy.13.wr_ref, ...), custom_call_target="tpu_custom_call" | custom-call | tf_op jit(solution)/shard_map/pallas_call | solution.py:319
  18.4 0.0 copy-start.1
  18.4 1.4 %copy_bitcast_fusion = (f32[16,4,32]{2,1,0:T(4,128)}, f32[16,4,32]{2,1,0:T(4,128)}) fusion(f32[4,16,32]{2,1,0:T(8,128)} %bitcast.9, f32[4,16,32]{2,1,0:T(8,128)} %bitcast.8), kind=kLoop, calls=%fused_computation | loop fusion | bytes 32768 | tf_op jit(solution)/shard_map/transpose | solution.py:354
  19.8 0.0 copy-done.1
  19.8 0.6 %copy.19 = bf16[4,16,128]{2,1,0:T(8,128)(2,1)} copy(bf16[4,16,128]{2,1,0:T(8,128)(2,1)S(1)} %copy-done.1) | data formatting | bytes 32768
Async XLA Ops:
  0.6 0.7 %copy-start.2 = (s32[16,4]{0,1:T(4,128)S(1)}, s32[16,4]{0,1:T(4,128)}, u32[]{:S(2)}) copy-start(s32[16,4]{0,1:T(4,128)} %param.9) | copy-start | bytes 772
  2.0 1.5 %copy-start = (bf16[256,32]{0,1:T(8,128)(2,1)S(1)}, bf16[256,32]{0,1:T(8,128)(2,1)}, u32[]{:S(2)}) copy-start(bf16[256,32]{0,1:T(8,128)(2,1)} %param.12) | copy-start | bytes 49156
  18.4 1.4 %copy-start.1 = (bf16[4,16,128]{2,1,0:T(8,128)(2,1)S(1)}, bf16[4,16,128]{2,1,0:T(8,128)(2,1)}, u32[]{:S(2)}) copy-start(bf16[4,16,128]{2,1,0:T(8,128)(2,1)} %get-tuple-element.14) | copy-start | bytes 49156

commit v2 on v1

--- a/solution.py
+++ b/solution.py
@@ -34,14 +34,16 @@
 
 def kernel(
     nrow,
+    x_hbm, am_hbm, rm_hbm, wl_hbm, wr_hbm, w_hbm, bias_hbm, cot_hbm,
+    pu_hbm, lg_hbm, rg_hbm,
     x_ref, am_ref, rm_ref, wl_ref, wr_ref, w_ref, bias_ref, cot_ref,
     pu_ref, lg_ref, rg_ref,
     g_s, gp_r, f_s, l_r, r_r, ro_r, ct_s, ct_r, cf_r, m_s, m_r,
     w32, a32, b32, o32, c32, p2, q2,
-    ssem, rsem, psem,
+    ssem, rsem, psem, isem, osem,
 ):
     seq, loc, feat = x_ref.shape
-    proj = wl_ref.shape[1]
+    proj = wl_ref.shape[0]
     half_res, chan = cot_ref.shape[1], cot_ref.shape[2]
     res = nrow * loc
     per_half = half_res // loc
@@ -75,16 +77,39 @@
                 pl.semaphore_signal(barrier, inc=1, device_id=dev(r, col), device_id_type=MESH)
 
     each(nrow, greet)
+    loads = [
+        pltpu.make_async_copy(src, dst, isem.at[k])
+        for k, (src, dst) in enumerate(
+            (
+                (x_hbm, x_ref), (wl_hbm, wl_ref), (wr_hbm, wr_ref), (am_hbm, am_ref),
+                (rm_hbm, rm_ref), (cot_hbm, cot_ref), (w_hbm, w_ref), (bias_hbm, bias_ref),
+            )
+        )
+    ]
+    for load in loads:
+        load.start()
+    for load in loads[:6]:
+        load.wait()
 
     xf = x_ref[...].astype(F32)
     x = jnp.concatenate([xf[:, r, :] for r in range(loc)], axis=0).astype(BF16)
     live = jnp.concatenate(
-        [(am_ref[:, r : r + 1] * rm_ref[:, r : r + 1]).astype(F32) for r in range(loc)], axis=0
-    )
+        [
+            jnp.broadcast_to(
+                (am_ref[r : r + 1, :] * rm_ref[:, r : r + 1]).astype(F32), (seq, seq)
+            )
+            for r in range(loc)
+        ],
+        axis=0,
+    )
+    diagonal = (iota((rows, seq), 0) & (seq - 1)) == iota((rows, seq), 1)
+    live = jnp.sum(jnp.where(diagonal, live, 0.0), axis=1, keepdims=True)
     live = jnp.broadcast_to(live, (rows, 128))
-    left = mm(x, wl_ref[...])
-    right = mm(x, wr_ref[...])
-    both = jnp.concatenate([left, right, jnp.ones((rows, 128 - 2 * proj), F32)], axis=1) * live
+    factors = jnp.concatenate(
+        [wl_ref[...], wr_ref[...], jnp.zeros((128 - 2 * proj, feat), BF16)], axis=0
+    )
+    both = lax.dot_general(x, factors, (((1,), (1,)), ((), ())), preferred_element_type=F32)
+    both = jnp.where(iota((rows, 128), 1) < 2 * proj, both, 1.0) * live
     g = both.astype(BF16)
     g_s[...] = g
     lane = iota((rows, 128), 1)
@@ -182,6 +207,8 @@
     def _():
         ct_r[row] = ct_s[jnp.where(row >= per_half, row - per_half, row)]
 
+    loads[6].wait()
+    loads[7].wait()
     w32[...] = w_ref[...].astype(F32)
     w_c = jnp.concatenate(
         [w32[pl.ds(e, proj, stride=proj), :] for e in range(proj)], axis=1
@@ -276,6 +303,12 @@
         div = w32[pl.ds(pl.multiple_of(col * half_res, half_res), half_res), :]
         pu_ref[i] = (mapped[:, i * chan : (i + 1) * chan] / div + bias).astype(BF16)
 
+    stores = [
+        pltpu.make_async_copy(src, dst, osem.at[k])
+        for k, (src, dst) in enumerate(((pu_ref, pu_hbm), (lg_ref, lg_hbm), (rg_ref, rg_hbm)))
+    ]
+    stores[0].start()
+
     def grad(flat, scaled, weight):
         q = lax.dot_general(
             flat, scaled, (((0,), (0,)), ((), ())), preferred_element_type=F32
@@ -293,6 +326,7 @@
         [(cf_r[i].astype(F32) / counts[i]).astype(BF16) for i in range(loc)], axis=1
     )
     lg_ref[...] = grad(right_all, scaled, w_c)
+    stores[1].start()
     scaled_t = jnp.concatenate(
         [
             (c32[pl.ds(j, res, stride=loc), :] / counts[j]).astype(BF16)
@@ -301,10 +335,13 @@
         axis=1,
     )
     rg_ref[...] = grad(left_all, scaled_t, w_e)
+    stores[2].start()
 
     partner(0).wait_send()
     partner(1).wait_send()
     each(nrow, lambda j: sends(nrow - 1 - j, lambda d: d.wait_send()))
+    for store in stores:
+        store.wait()
 
 
 def per_device(nrow, x, am, rm, wl, wr, w, bias, cot):
@@ -315,7 +352,8 @@
     tiles = proj * seq // 128
     fr = loc * tiles
     rows = loc * seq
-    vm = pl.BlockSpec(memory_space=pltpu.VMEM)
+    hbm = pl.BlockSpec(memory_space=pl.ANY)
+    operands = (x, am.T, rm.reshape(1, loc), wl.T, wr.T, w, bias.reshape(1, chan), cot)
     pu, lg, rg = pl.pallas_call(
         functools.partial(kernel, nrow),
         out_shape=(
@@ -323,9 +361,13 @@
             jax.ShapeDtypeStruct((rows, proj), F32),
             jax.ShapeDtypeStruct((rows, proj), F32),
         ),
-        in_specs=[vm] * 8,
-        out_specs=(vm, vm, vm),
-        scratch_shapes=[
+        in_specs=[hbm] * 8,
+        out_specs=(hbm, hbm, hbm),
+        scratch_shapes=[pltpu.VMEM(a.shape, a.dtype) for a in operands]
+        + [
+            pltpu.VMEM(cot.shape, BF16),
+            pltpu.VMEM((rows, proj), F32),
+            pltpu.VMEM((rows, proj), F32),
             pltpu.VMEM((rows, 128), BF16),
             pltpu.VMEM((rows, 128), BF16),
             pltpu.VMEM((2, fr, 128), BF16),
@@ -347,9 +389,11 @@
             pltpu.SemaphoreType.DMA((7, nrow)),
             pltpu.SemaphoreType.DMA((7, nrow)),
             pltpu.SemaphoreType.DMA((4,)),
+            pltpu.SemaphoreType.DMA((8,)),
+            pltpu.SemaphoreType.DMA((3,)),
         ],
         compiler_params=pltpu.CompilerParams(collective_id=0, has_side_effects=True),
-    )(x, am, rm.reshape(1, loc), wl, wr, w, bias.reshape(1, chan), cot)
+    )(*operands)
     lg = jnp.swapaxes(lg.reshape(loc, seq, proj), 0, 1)
     rg = jnp.swapaxes(rg.reshape(loc, seq, proj), 0, 1)
     return pu, lg, rg

time: 20.7 us -> 16.4 us (0.79)
  local copies, waits for them, and re-layouts: 5.58 us -> 2.03 us
  Pallas kernels: 14.2 us -> 13.5 us
    unnamed x10 -> x3, local copies, waits for them, and re-layouts: 4.15 us -> 0.61 us
    pallas_call x1, Pallas kernels: 14.2 us -> 13.5 us  [per_device(): pl.pallas_call(functools.partial(kernel, nrow), out_shape=(jax.ShapeDtype...]
where the time goes in v2:
time: 16.4 us; the launch traced here: 16.2 us
  Pallas kernels  13.5 us (82%)
  local copies, waits for them, and re-layouts  2.03 us (12%)
  between operations  0.65 us (4%)
    pallas_call x1, Pallas kernels, per_device(): pl.pallas_call(functools.partial(kernel, nrow), out_shape=(jax.ShapeDtype...  13.5 us
    transpose x1, local copies, waits for them, and re-layouts, per_device(): rg = jnp.swapaxes(rg.reshape(loc, seq, proj), 0, 1)  1.42 us
    unnamed x3, local copies, waits for them, and re-layouts  0.61 us

profile of v2, /device:TPU:0, one launch (start us, length us, event | category | flops | bytes accessed | tf_op | source)
XLA Modules:
  0.0 16.2 jit_solution(217368164833764140)
XLA Ops:
  0.6 13.5 %shard_map.103 = (bf16[4,16,128]{2,1,0:T(8,128)(2,1)}, f32[64,32]{1,0:T(8,128)}, f32[64,32]{1,0:T(8,128)}) custom-call(bf16[16,4,256]{2,1,0:T(4,128)(2,1)} %x_hbm.1, s32[4,16]{1,0:T(4,128)} %bitcast.15, s32[1,4]{1,0:T(1,128)} %bitcast.16, bf16[32,256]{1,0:T(8,128)(2,1)} %bitcast.13, bf16[32,256]{1,0:T(8,128)(2,1)} %bitcast.14, bf16[1024,128]{1,0:T(8,128)(2,1)} %w_hbm.1, ...), custom_call_target="tpu_custom_call" | custom-call | tf_op jit(solution)/shard_map/pallas_call | solution.py:357
  14.1 0.0 copy-start
  14.1 1.4 %copy_bitcast_fusion = (f32[16,4,32]{2,1,0:T(4,128)}, f32[16,4,32]{2,1,0:T(4,128)}) fusion(f32[4,16,32]{2,1,0:T(8,128)} %bitcast.12, f32[4,16,32]{2,1,0:T(8,128)} %bitcast.11), kind=kLoop, calls=%fused_computation | loop fusion | bytes 32768 | tf_op jit(solution)/shard_map/transpose | solution.py:398
  15.6 0.0 copy-done
  15.6 0.6 %copy.16 = bf16[4,16,128]{2,1,0:T(8,128)(2,1)} copy(bf16[4,16,128]{2,1,0:T(8,128)(2,1)S(1)} %copy-done) | data formatting | bytes 32768
Async XLA Ops:
  14.1 1.4 %copy-start = (bf16[4,16,128]{2,1,0:T(8,128)(2,1)S(1)}, bf16[4,16,128]{2,1,0:T(8,128)(2,1)}, u32[]{:S(2)}) copy-start(bf16[4,16,128]{2,1,0:T(8,128)(2,1)} %get-tuple-element.14) | copy-start | bytes 49156
